TPU v7x, 32 devices: a whole 2x2x4 slice. The times are simulated.
32 devices in a mesh: groups: 2 (over x), stem: 8 (over z, y), cuts: 2 (over core).
Axes of the slice: x: 2, y: 2, z: 4, core: 2. Of those that a mesh axis runs over, the one named last changes fastest.
Arguments:
- stem: bfloat16 [4, 2, 4096, 1024], P(('groups', 'cuts'), None, 'stem'), parts along dimension 0, may hold values from -6 to 6
- edge_values: int32 [4, 4], P(('groups', 'cuts')), parts along dimension 0, may hold values from 0 to 1
- index_order: int32 [1024], replicated, may hold values from 0 to 1023, each once
- branch_first: bfloat16 [2, 1024, 1024], replicated, may hold values from -0.125 to 0.125
- branch_second: bfloat16 [2, 1024, 1024], replicated, may hold values from -0.125 to 0.125
- branch_third: bfloat16 [2, 1024, 256], replicated, may hold values from -0.125 to 0.125
- edge_table: float32 [16, 2, 256], replicated, may hold values from -6 to 6
- picks: int32 [4096], P('stem'), may hold values from 0 to 511, as said below
Outputs:
- amplitudes: float32 [2, 8192, 256], P(None, ('groups', 'stem')), parts along dimension 1
There are 2 independent parts, one for each index of `groups`. A program takes and returns all parts, laid end to end along the dimension named above; an argument that names none is the same for every part. Nothing has to cross between parts.
Inputs may be any that keep to these rules, and one draw needn't show every extreme that they name: `index_order`: each number of 0 to 1023 once. `picks`: each aligned block of 512 entries names every number of 0 to 511 once.
All inputs are finite; a program needn't handle non-finite values.
Results may differ from a plain program's by a relative error of at most 0.0041.
Values may be sent and summed in bfloat16 or wider, within the bound.
No kernel may reach another device: no remote copies, remote signals or barrier semaphores. Data moves between devices by JAX's collectives and lax.ppermute only.
A program may use at most 64 MiB of HBM per device.

v0:
```python
import jax
import jax.numpy as jnp
from jax import lax
from jax.sharding import PartitionSpec as P


def swapped(value, axis, distance):
    mask = 2**distance
    pairs = [(source, source ^ mask) for source in range(lax.axis_size(axis))]
    return lax.ppermute(value, axis, pairs)


def complex_dot(operand, matrix):
    real = jnp.dot(operand[0], matrix[0], preferred_element_type=jnp.float32) - jnp.dot(
        operand[1], matrix[1], preferred_element_type=jnp.float32
    )
    imag = jnp.dot(operand[0], matrix[1], preferred_element_type=jnp.float32) + jnp.dot(
        operand[1], matrix[0], preferred_element_type=jnp.float32
    )
    return jnp.stack([real, imag])


def on_device(
    stem, edge_values, index_order, branch_first, branch_second, branch_third, edge_table, picks
):
    stem_size = lax.axis_size("stem")
    bit_pos = stem_size.bit_length() - 2
    top_bit = lax.axis_index("stem") // (stem_size // 2) % 2
    is_low = top_bit == 0
    width = branch_first.shape[1]
    half_width = width // 2
    rows_dev = stem.shape[2]
    block_rows = rows_dev // stem_size
    inverse = jnp.zeros_like(index_order).at[index_order].set(jnp.arange(width, dtype=jnp.int32))
    reordered = jnp.take(branch_second, inverse, axis=1)
    powers = 2 ** jnp.arange(edge_values.shape[1], dtype=jnp.int32)
    codes = jnp.arange(edge_table.shape[0], dtype=jnp.int32)
    first = complex_dot(stem[0], branch_first).astype(jnp.bfloat16)
    low_half = first[:, :, :half_width]
    high_half = first[:, :, half_width:]
    outgoing = jnp.where(is_low, high_half, low_half)
    incoming = swapped(outgoing, "stem", bit_pos)
    joined = jnp.where(
        is_low,
        jnp.concatenate([low_half, incoming], axis=2),
        jnp.concatenate([incoming, high_half], axis=2),
    )
    second = complex_dot(joined, reordered).astype(jnp.bfloat16)
    contracted = complex_dot(second, branch_third)
    moved = lax.all_to_all(
        contracted.reshape(2, stem_size, block_rows, contracted.shape[2]),
        "stem",
        split_axis=1,
        concat_axis=1,
        tiled=True,
    )
    third = jnp.take(moved.reshape(2, rows_dev, contracted.shape[2]), picks, axis=1)
    code = jnp.sum(edge_values[0] * powers)
    onehot = (codes == code).astype(jnp.float32)
    factor = jnp.sum(onehot[:, None, None] * edge_table, axis=0)
    real = third[0] * factor[0][None, :] - third[1] * factor[1][None, :]
    imag = third[0] * factor[1][None, :] + third[1] * factor[0][None, :]
    total = jnp.stack([real, imag])
    return lax.psum(total, "cuts")


def solution(mesh):
    return jax.shard_map(
        on_device,
        mesh=mesh,
        in_specs=(
            P(("groups", "cuts"), None, "stem", None),
            P(("groups", "cuts"), None),
            P(),
            P(),
            P(),
            P(),
            P(),
            P("stem"),
        ),
        out_specs=P(None, ("groups", "stem"), None),
        check_vma=False,
    )
```

profile of v0, /device:TPU:0, one launch (start us, length us, event | category | flops | bytes accessed | tf_op | source)
XLA Modules:
  0.0 144.1 jit_solution(4913342444032320021)
XLA Ops:
  6.5 0.0 copy-start.4
  6.5 0.0 copy-start.6
  6.5 4.6 %fusion.2 = f32[512,1024]{1,0:T(8,128)} fusion(bf16[2,1024,1024]{2,1,0:T(8,128)(2,1)} %param.11, bf16[1,2,512,1024]{3,2,1,0:T(8,128)(2,1)} %param.8), kind=kOutput, calls=%fused_computation.11 | convolution fusion | flops 1073741824 | bytes 5242880 | tf_op jit(solution)/shard_map/dot_general | solution.py:14
  11.2 0.0 copy-done.4
  11.2 0.0 copy-done.6
  11.2 2.6 %fusion = f32[512,1024]{1,0:T(8,128)} fusion(bf16[2,1024,1024]{2,1,0:T(8,128)(2,1)S(1)} %copy-done.4, bf16[1,2,512,1024]{3,2,1,0:T(8,128)(2,1)S(1)} %copy-done.6), kind=kOutput, calls=%fused_computation.9 | convolution fusion | flops 1073741824 | bytes 5242880 | tf_op jit(solution)/shard_map/dot_general | solution.py:17
  13.8 0.0 copy-start.5
  13.8 0.0 copy-start.8
  13.8 3.6 %fusion.20 = bf16[1,512,1024]{2,1,0:T(8,128)(2,1)S(1)} fusion(f32[512,1024]{1,0:T(8,128)} %fusion.2, bf16[2,1024,1024]{2,1,0:T(8,128)(2,1)} %param.11, bf16[1,2,512,1024]{3,2,1,0:T(8,128)(2,1)S(1)} %copy-done.6), kind=kOutput, calls=%fused_computation.29 | convolution fusion | flops 1074790400 | bytes 6291456 | tf_op jit(solution)/shard_map/dot_general | solution.py:14
  17.4 0.0 copy-done.5
  17.4 0.5 copy-done.8
  17.9 1.3 fusion.23
  19.2 0.0 copy-start.3
  19.2 0.5 broadcast_select_fusion
  19.7 4.1 %collective-permute-start = (bf16[2,512,512]{2,1,0:T(8,128)(2,1)S(1)}, bf16[2,512,512]{2,1,0:T(8,128)(2,1)}, u32[]{:S(2)}, u32[]{:S(2)}) collective-permute-start(bf16[2,512,512]{2,1,0:T(8,128)(2,1)S(1)} %get-tuple-element.5), channel_id=1, source_target_pairs={{0,8},{2,10},{4,12},{6,14},{8,0},{10,2},{12,4},{14,6},{1,9},{3,11}... | collective-permute-start | bytes 3145736 | tf_op jit(solution)/shard_map/ppermute | solution.py:10
  23.8 0.0 copy-done.3
  23.8 4.5 %scatter_custom_fusion = s32[1024]{0:T(1024)S(1)} fusion(s32[1024]{0:T(1024)S(1)} %compare_select_fusion.1, s32[1024]{0:T(1024)S(1)} %iota.11, s32[]{:T(128)} %constant.69.clone.1), kind=kCustom, calls=%fused_computation.69 | custom fusion | bytes 4100 | tf_op jit(solution)/shard_map/scatter | solution.py:34
  28.3 27.6 %gather_fusion = bf16[1024,2,1024]{2,0,1:T(8,128)(2,1)} fusion(bf16[2,1024,1024]{2,1,0:T(8,128)(2,1)} %param.12, s32[1024]{0:T(1024)S(1)} %fusion.46), kind=kCustom, calls=%fused_computation | custom fusion | bytes 8392704 | tf_op jit(solution)/shard_map/jit(_take)/gather | solution.py:35
  56.0 2.6 %select_bitcast_fusion = bf16[2,1024,1024]{2,1,0:T(8,128)(2,1)S(1)} fusion(bf16[1024,2,1024]{2,0,1:T(8,128)(2,1)} %gather_fusion, pred[1024]{0:T(1024)(128)(4,1)S(1)} %compare_and_fusion), kind=kLoop, calls=%fused_computation.3 | loop fusion | flops 2097152 | bytes 8389632 | tf_op jit(solution)/shard_map/jit(_take)/select_n | solution.py:35
  58.6 10.9 %collective-permute-done = bf16[2,512,512]{2,1,0:T(8,128)(2,1)} collective-permute-done((bf16[2,512,512]{2,1,0:T(8,128)(2,1)S(1)}, bf16[2,512,512]{2,1,0:T(8,128)(2,1)}, u32[]{:S(2)}, u32[]{:S(2)}) %collective-permute-start) | collective-permute-done | bytes 1048608 | tf_op jit(solution)/shard_map/ppermute | solution.py:10
  69.6 2.2 %maximum_select_fusion = bf16[2,512,1024]{2,1,0:T(8,128)(2,1)S(1)} fusion(bf16[2,512,512]{2,1,0:T(8,128)(2,1)} %collective-permute-done, bf16[2,512,512]{2,1,0:T(8,128)(2,1)S(1)} %get-tuple-element.6, bf16[2,512,512]{2,1,0:T(8,128)(2,1)S(1)} %get-tuple-element.7, pred[]{:T(512)S(6)} %eq.15), kind=kLoop, calls=%fused_computation.8 | loop fusion | flops 9437184 | bytes 5242881 | tf_op jit(solution)/shard_map/jit(_where)/select_n | solution.py:43
  71.8 1.3 fusion.8
  73.1 1.3 fusion.11
  74.3 0.0 copy-start
  74.3 1.3 subtract_convert_fusion
  75.6 0.0 copy-done
  75.6 0.4 fusion.40
  76.1 0.5 fusion.36
  76.6 1.3 add_convert_fusion
  77.9 0.5 convolution_subtract_fusion
  78.3 0.5 convolution_add_fusion
  78.8 0.0 copy-start.7
  78.8 0.0 copy-start.2
  78.8 0.0 copy-start.1
  78.8 1.1 pad_maximum_fusion.1
  79.9 5.8 %all-to-all-start = ((f32[2,8,64,256]{3,2,0,1:T(8,128)}), f32[2,8,64,256]{3,2,0,1:T(8,128)S(1)}, u32[]{:S(2)}, u32[]{:S(2)}) async-start(f32[2,8,64,256]{3,2,0,1:T(8,128)} %pad_maximum_fusion.1), calls=%async_computation | async-start | bytes 2097152 | tf_op jit(solution)/shard_map/all_to_all | solution.py:50
  85.7 0.0 all-reduce.2.cloned.1.call-start
  85.7 0.0 copy-done.7
  85.7 0.6 fusion.52
  86.3 0.6 compare_convert_fusion
  86.9 0.0 copy-done.2
  86.9 0.0 copy-done.1
  87.0 0.1 multiply_reduce_fusion
  87.1 24.5 %all-to-all-done = f32[2,8,64,256]{3,2,0,1:T(8,128)S(1)} async-done(((f32[2,8,64,256]{3,2,0,1:T(8,128)}), f32[2,8,64,256]{3,2,0,1:T(8,128)S(1)}, u32[]{:S(2)}, u32[]{:S(2)}) %all-to-all-start) | async-done | bytes 1048608 | tf_op jit(solution)/shard_map/all_to_all | solution.py:50
  111.6 0.8 copy.17
  112.4 2.6 %gather_fusion.1 = f32[512,2,256]{2,1,0:T(2,128)S(1)} fusion(f32[2,512,256]{2,0,1:T(2,128)S(1)} %bitcast.83, s32[1024]{0:T(1024)S(1)} %pad_clamp_fusion), kind=kCustom, calls=%fused_computation.1 | custom fusion | bytes 2099200 | tf_op jit(solution)/shard_map/jit(_take)/gather | solution.py:57
  115.0 0.2 fusion.31
  115.2 0.1 multiply_subtract_fusion
  115.3 1.0 pad_maximum_fusion.2
  116.3 0.0 all-reduce.2.cloned.1.call-update
  116.3 18.6 %all-reduce.2.cloned.1.call-done = f32[2,512,256]{2,1,0:T(8,128)} async-done(((f32[2,512,256]{2,1,0:T(8,128)}), f32[2,512,256]{2,1,0:T(8,128)}) %all-reduce.2.cloned.1.call-update) | async-done | bytes 1048592 | tf_op jit(solution)/shard_map/psum | solution.py:64
  135.0 2.3 %copy.23 = f32[2,512,256]{2,1,0:T(8,128)} copy(f32[2,512,256]{2,1,0:T(8,128)} %all-reduce.2.cloned.1.call-done) | data formatting | bytes 2097152
  (8 shorter events, 0.0 us)
Async XLA Ops:
  6.5 4.6 %copy-start.4 = (bf16[2,1024,1024]{2,1,0:T(8,128)(2,1)S(1)}, bf16[2,1024,1024]{2,1,0:T(8,128)(2,1)}, u32[]{:S(2)}) copy-start(bf16[2,1024,1024]{2,1,0:T(8,128)(2,1)} %param.11) | copy-start | bytes 12582916
  6.5 4.6 %copy-start.6 = (bf16[1,2,512,1024]{3,2,1,0:T(8,128)(2,1)S(1)}, bf16[1,2,512,1024]{3,2,1,0:T(8,128)(2,1)}, u32[]{:S(2)}) copy-start(bf16[1,2,512,1024]{3,2,1,0:T(8,128)(2,1)} %param.8) | copy-start | bytes 6291460
  13.8 3.6 %copy-start.5 = (bf16[2,1024,1024]{2,1,0:T(8,128)(2,1)S(1)}, bf16[2,1024,1024]{2,1,0:T(8,128)(2,1)}, u32[]{:S(2)}) copy-start(bf16[2,1024,1024]{2,1,0:T(8,128)(2,1)} %param.11) | copy-start | bytes 12582916
  13.8 4.1 %copy-start.8 = (f32[512,1024]{1,0:T(8,128)S(1)}, f32[512,1024]{1,0:T(8,128)}, u32[]{:S(2)}) copy-start(f32[512,1024]{1,0:T(8,128)} %fusion) | copy-start | bytes 6291460
  19.2 4.6 %copy-start.3 = (s32[1024]{0:T(1024)S(1)}, s32[1024]{0:T(1024)}, u32[]{:S(2)}) copy-start(s32[1024]{0:T(1024)} %param.10) | copy-start | bytes 12292
  19.7 49.9 %collective-permute-start = (bf16[2,512,512]{2,1,0:T(8,128)(2,1)S(1)}, bf16[2,512,512]{2,1,0:T(8,128)(2,1)}, u32[]{:S(2)}, u32[]{:S(2)}) collective-permute-start(bf16[2,512,512]{2,1,0:T(8,128)(2,1)S(1)} %get-tuple-element.5), channel_id=1, source_target_pairs={{0,8},{2,10},{4,12},{6,14},{8,0},{10,2},{12,4},{14,6},{1,9},{3,11}... | collective-permute-start | bytes 3145736 | tf_op jit(solution)/shard_map/ppermute | solution.py:10
  74.3 1.3 copy-start
  78.8 6.9 %copy-start.7 = (s32[1,4]{1,0:T(1,128)S(1)}, s32[1,4]{1,0:T(1,128)}, u32[]{:S(2)}) copy-start(s32[1,4]{1,0:T(1,128)} %param.9) | copy-start | bytes 52
  78.8 8.1 %copy-start.2 = (s32[512]{0:T(512)S(1)}, s32[512]{0:T(512)}, u32[]{:S(2)}) copy-start(s32[512]{0:T(512)} %param.15) | copy-start | bytes 6148
  78.8 8.1 %copy-start.1 = (f32[16,2,256]{2,1,0:T(2,128)S(1)}, f32[16,2,256]{2,1,0:T(2,128)}, u32[]{:S(2)}) copy-start(f32[16,2,256]{2,1,0:T(2,128)} %param.14) | copy-start | bytes 98308
  79.9 31.7 %all-to-all-start = ((f32[2,8,64,256]{3,2,0,1:T(8,128)}), f32[2,8,64,256]{3,2,0,1:T(8,128)S(1)}, u32[]{:S(2)}, u32[]{:S(2)}) async-start(f32[2,8,64,256]{3,2,0,1:T(8,128)} %pad_maximum_fusion.1), calls=%async_computation | async-start | bytes 2097152 | tf_op jit(solution)/shard_map/all_to_all | solution.py:50
  85.7 49.3 %all-reduce.2.cloned.1.call-start = ((), (), s32[]{:S(2)}) async-start(), calls=%async_computation.1 | async-start | bytes 2097152 | tf_op jit(solution)/shard_map/psum | solution.py:64
Sparse Core Ops, SparseCore 0:
  116.5 18.4 all-reduce.1
where the time goes:
time: 145 us; the launch traced here: 144 us
  waiting for transfers between devices  54.1 us (37%)
  local copies, waits for them, and re-layouts  38.3 us (26%)
  matrix products  19.1 us (13%)
  between operations  13.7 us (9%)
  starting transfers between devices  9.93 us (7%)
  other arithmetic  9.01 us (6%)
    gather x1, local copies, waits for them, and re-layouts, on_device(): reordered = jnp.take(branch_second, inverse, axis=1)  27.6 us
    all_to_all x1, waiting for transfers between devices, on_device(): lax.all_to_all(contracted.reshape(2, stem_size, block_rows, contracted.sh...  24.5 us
    psum x1, waiting for transfers between devices, on_device(): return lax.psum(total, 'cuts')  18.6 us
    ppermute x1, waiting for transfers between devices, swapped(): return lax.ppermute(value, axis, pairs)  10.9 us
    dot_general x3, matrix products, complex_dot(): jnp.dot(operand[1], matrix[1], preferred_element_type=jnp.float32)  6.33 us
    all_to_all x1, starting transfers between devices, on_device(): lax.all_to_all(contracted.reshape(2, stem_size, block_rows, contracted.sh...  5.77 us
    dot_general x3, matrix products, complex_dot(): jnp.dot(operand[0], matrix[0], preferred_element_type=jnp.float32)  5.36 us
    scatter x1, local copies, waits for them, and re-layouts, on_device(): jnp.zeros_like(index_order).at[index_order]  4.49 us
  transfers between devices with their start and end apart: 3, of which 3 were waited for; matrix products, arithmetic and copies ran while one was open for 25% of the time, Pallas kernels for 0%

commit v1 on v0

--- a/solution.py
+++ b/solution.py
@@ -2,6 +2,19 @@
 import jax.numpy as jnp
 from jax import lax
 from jax.sharding import PartitionSpec as P
+
+
+def prepare_strips_all_here(incoming_x, array_axis, arr):
+    row_out, main = (incoming_x.shape[:array_axis], incoming_x.shape[array_axis + 1 :])
+    return jnp.moveaxis(incoming_x.reshape(*row_out, arr, -1, *main), array_axis, 0)
+
+
+def carry_matrix(field, at_axis):
+    field = jnp.moveaxis(field, 0, at_axis)
+    u_next = field.shape
+    return field.reshape(
+        *u_next[:at_axis], u_next[at_axis] * u_next[at_axis + 1], *u_next[at_axis + 2 :]
+    )
 
 
 def swapped(value, axis, distance):
@@ -23,6 +36,20 @@
 def on_device(
     stem, edge_values, index_order, branch_first, branch_second, branch_third, edge_table, picks
 ):
+
+    def clear_signs_over_axis(inputs, ax_name, here_x, body):
+        carry, small = (lax.axis_size(ax_name), lax.axis_index(ax_name))
+        arr_now = prepare_strips_all_here(inputs, here_x, carry)
+        val2 = arr_now
+        for p in range(1, carry):
+            shaped, reply = ((small + p) % carry, (small - p) % carry)
+            parts_out = lax.dynamic_index_in_dim(arr_now, shaped, 0)
+            known = lax.ppermute(
+                parts_out, ax_name, [(ii, (ii + p) % carry) for ii in range(carry)]
+            )
+            val2 = lax.dynamic_update_slice_in_dim(val2, known, reply, axis=0)
+        return carry_matrix(val2, body)
+
     stem_size = lax.axis_size("stem")
     bit_pos = stem_size.bit_length() - 2
     top_bit = lax.axis_index("stem") // (stem_size // 2) % 2
@@ -47,12 +74,8 @@
     )
     second = complex_dot(joined, reordered).astype(jnp.bfloat16)
     contracted = complex_dot(second, branch_third)
-    moved = lax.all_to_all(
-        contracted.reshape(2, stem_size, block_rows, contracted.shape[2]),
-        "stem",
-        split_axis=1,
-        concat_axis=1,
-        tiled=True,
+    moved = clear_signs_over_axis(
+        contracted.reshape(2, stem_size, block_rows, contracted.shape[2]), "stem", 1, 1
     )
     third = jnp.take(moved.reshape(2, rows_dev, contracted.shape[2]), picks, axis=1)
     code = jnp.sum(edge_values[0] * powers)

time: 145 us -> 140 us (0.966)
  waiting for transfers between devices: 54.1 us -> 41.2 us
  starting transfers between devices: 9.93 us -> 18.2 us
    all_to_all x1 -> x0, waiting for transfers between devices: 24.5 us -> none  [on_device(): lax.all_to_all(contracted.reshape(2, stem_size, block_rows, contracted.sh...]
    ppermute x0 -> x7, starting transfers between devices: none -> 14.1 us  [clear_signs_over_axis(): lax.ppermute(parts_out, ax_name, [(ii, (ii + p) % carry) for ii in range(...]
    ppermute x0 -> x7, waiting for transfers between devices: none -> 8.56 us  [clear_signs_over_axis(): lax.ppermute(parts_out, ax_name, [(ii, (ii + p) % carry) for ii in range(...]
    all_to_all x1 -> x0, starting transfers between devices: 5.77 us -> none  [on_device(): lax.all_to_all(contracted.reshape(2, stem_size, block_rows, contracted.sh...]
    psum x1, waiting for transfers between devices: 18.6 us -> 23.5 us  [on_device(): return lax.psum(total, 'cuts')]
    ppermute x1, waiting for transfers between devices: 10.9 us -> 9.17 us  [swapped(): return lax.ppermute(value, axis, pairs)]
  transfers between devices with their start and end apart: 3 -> 9, of which waited for: 3 -> 6; matrix products, arithmetic and copies ran while one was open for 25% -> 26% of each run, Pallas kernels for 0% -> 0%
where the time goes in v1:
time: 140 us; the launch traced here: 139 us
  waiting for transfers between devices  41.2 us (29%)
  local copies, waits for them, and re-layouts  38.5 us (28%)
  matrix products  19 us (14%)
  starting transfers between devices  18.2 us (13%)
  between operations  14 us (10%)
  other arithmetic  8.09 us (6%)
    gather x1, local copies, waits for them, and re-layouts, on_device(): reordered = jnp.take(branch_second, inverse, axis=1)  27.7 us
    psum x1, waiting for transfers between devices, on_device(): return lax.psum(total, 'cuts')  23.5 us
    ppermute x7, starting transfers between devices, clear_signs_over_axis(): lax.ppermute(parts_out, ax_name, [(ii, (ii + p) % carry) for ii in range(...  14.1 us
    ppermute x1, waiting for transfers between devices, swapped(): return lax.ppermute(value, axis, pairs)  9.17 us
    ppermute x7, waiting for transfers between devices, clear_signs_over_axis(): lax.ppermute(parts_out, ax_name, [(ii, (ii + p) % carry) for ii in range(...  8.56 us
    dot_general x3, matrix products, complex_dot(): jnp.dot(operand[1], matrix[1], preferred_element_type=jnp.float32)  6.33 us
    dot_general x3, matrix products, complex_dot(): jnp.dot(operand[0], matrix[0], preferred_element_type=jnp.float32)  5.34 us
    scatter x1, local copies, waits for them, and re-layouts, on_device(): jnp.zeros_like(index_order).at[index_order]  4.49 us
  transfers between devices with their start and end apart: 9, of which 6 were waited for; matrix products, arithmetic and copies ran while one was open for 26% of the time, Pallas kernels for 0%

profile of v1, /device:TPU:0, one launch (start us, length us, event | category | flops | bytes accessed | tf_op | source)
XLA Modules:
  0.0 138.9 jit_solution(3341475410471258741)
XLA Ops:
  6.5 0.0 all-reduce.2.cloned.1.call-start
  6.5 0.0 copy-start.4
  6.5 0.0 copy-start.6
  6.5 4.6 %fusion.2 = f32[512,1024]{1,0:T(8,128)} fusion(bf16[2,1024,1024]{2,1,0:T(8,128)(2,1)} %param.11, bf16[1,2,512,1024]{3,2,1,0:T(8,128)(2,1)} %param.8), kind=kOutput, calls=%fused_computation.26 | convolution fusion | flops 1073741824 | bytes 5242880 | tf_op jit(solution)/shard_map/dot_general | solution.py:27
  11.2 0.0 copy-done.4
  11.2 0.0 copy-done.6
  11.2 2.6 %fusion = f32[512,1024]{1,0:T(8,128)} fusion(bf16[2,1024,1024]{2,1,0:T(8,128)(2,1)S(1)} %copy-done.4, bf16[1,2,512,1024]{3,2,1,0:T(8,128)(2,1)S(1)} %copy-done.6), kind=kOutput, calls=%fused_computation.24 | convolution fusion | flops 1073741824 | bytes 5242880 | tf_op jit(solution)/shard_map/dot_general | solution.py:30
  13.7 0.0 copy-start.5
  13.7 3.6 %fusion.20 = bf16[1,512,1024]{2,1,0:T(8,128)(2,1)S(1)} fusion(f32[512,1024]{1,0:T(8,128)} %fusion.2, bf16[2,1024,1024]{2,1,0:T(8,128)(2,1)} %param.11, bf16[1,2,512,1024]{3,2,1,0:T(8,128)(2,1)S(1)} %copy-done.6), kind=kOutput, calls=%fused_computation.44 | convolution fusion | flops 1074790400 | bytes 6291456 | tf_op jit(solution)/shard_map/dot_general | solution.py:27
  17.4 0.0 copy-done.5
  17.4 0.5 copy-done.8
  17.9 1.3 fusion.23
  19.2 0.0 copy-start.2
  19.2 0.0 copy-start.3
  19.2 0.0 copy-start.7
  19.2 0.5 broadcast_select_fusion
  19.7 4.1 %collective-permute-start = (bf16[2,512,512]{2,1,0:T(8,128)(2,1)S(1)}, bf16[2,512,512]{2,1,0:T(8,128)(2,1)}, u32[]{:S(2)}, u32[]{:S(2)}) collective-permute-start(bf16[2,512,512]{2,1,0:T(8,128)(2,1)S(1)} %get-tuple-element.5), channel_id=1, source_target_pairs={{0,8},{2,10},{4,12},{6,14},{8,0},{10,2},{12,4},{14,6},{1,9},{3,11}... | collective-permute-start | bytes 3145736 | tf_op jit(solution)/shard_map/ppermute | solution.py:23
  23.8 0.0 copy-done.2
  23.8 0.0 copy-done.3
  23.8 4.5 %scatter_custom_fusion = s32[1024]{0:T(1024)S(1)} fusion(s32[1024]{0:T(1024)S(1)} %compare_select_fusion.1, s32[1024]{0:T(1024)S(1)} %iota.11, s32[]{:T(128)} %constant.156.clone.1), kind=kCustom, calls=%fused_computation.105 | custom fusion | bytes 4100 | tf_op jit(solution)/shard_map/scatter | solution.py:61
  28.4 0.0 copy-done.7
  28.4 0.6 fusion.67
  29.0 0.6 compare_convert_fusion
  29.9 0.0 copy-start.1
  29.9 27.7 %gather_fusion = bf16[1024,2,1024]{2,0,1:T(8,128)(2,1)} fusion(bf16[2,1024,1024]{2,1,0:T(8,128)(2,1)} %param.12, s32[1024]{0:T(1024)S(1)} %fusion.61), kind=kCustom, calls=%fused_computation | custom fusion | bytes 8392704 | tf_op jit(solution)/shard_map/jit(_take)/gather | solution.py:62
  57.6 0.0 copy-done.1
  57.6 0.1 multiply_reduce_fusion
  57.7 2.6 %select_bitcast_fusion = bf16[2,1024,1024]{2,1,0:T(8,128)(2,1)S(1)} fusion(bf16[1024,2,1024]{2,0,1:T(8,128)(2,1)} %gather_fusion, pred[1024]{0:T(1024)(128)(4,1)S(1)} %compare_and_fusion), kind=kLoop, calls=%fused_computation.3 | loop fusion | flops 2097152 | bytes 8389632 | tf_op jit(solution)/shard_map/jit(_take)/select_n | solution.py:62
  60.4 9.2 %collective-permute-done = bf16[2,512,512]{2,1,0:T(8,128)(2,1)} collective-permute-done((bf16[2,512,512]{2,1,0:T(8,128)(2,1)S(1)}, bf16[2,512,512]{2,1,0:T(8,128)(2,1)}, u32[]{:S(2)}, u32[]{:S(2)}) %collective-permute-start) | collective-permute-done | bytes 1048608 | tf_op jit(solution)/shard_map/ppermute | solution.py:23
  69.5 2.1 %maximum_select_fusion = bf16[2,512,1024]{2,1,0:T(8,128)(2,1)S(1)} fusion(bf16[2,512,512]{2,1,0:T(8,128)(2,1)} %collective-permute-done, bf16[2,512,512]{2,1,0:T(8,128)(2,1)S(1)} %get-tuple-element.6, bf16[2,512,512]{2,1,0:T(8,128)(2,1)S(1)} %get-tuple-element.7, pred[]{:T(512)S(6)} %eq.29), kind=kLoop, calls=%fused_computation.23 | loop fusion | flops 9437184 | bytes 5242881 | tf_op jit(solution)/shard_map/jit(_where)/select_n | solution.py:70
  71.7 1.3 fusion.8
  72.9 1.3 fusion.11
  74.2 0.0 copy-start
  74.2 1.3 subtract_convert_fusion
  75.5 0.0 copy-done
  75.5 0.4 fusion.41
  76.0 0.4 fusion.37
  76.4 1.3 add_convert_fusion
  77.7 0.5 convolution_subtract_fusion
  78.2 0.5 convolution_add_fusion
  78.6 0.1 fusion.60
  78.7 1.6 %collective-permute-start.1 = (f32[1,2,1,64,256]{4,3,0,2,1:T(8,128)S(1)}, f32[1,2,1,64,256]{4,3,0,2,1:T(8,128)S(1)}, u32[]{:S(2)}, u32[]{:S(2)}) collective-permute-start(f32[1,2,1,64,256]{4,3,0,2,1:T(8,128)S(1)} %get-tuple-element.11), channel_id=1, source_target_pairs={{0,2},{2,4},{4,6},{6,8},{8,10},{10,12},{12,14},{14,0},{1,3},{3,5},... | collective-permute-start | bytes 393224 | tf_op jit(solution)/shard_map/ppermute | solution.py:47
  80.3 0.1 fusion.27
  80.4 0.6 collective-permute-start.2
  81.0 3.3 %collective-permute-start.6 = (f32[1,2,1,64,256]{4,3,0,2,1:T(8,128)S(1)}, f32[1,2,1,64,256]{4,3,0,2,1:T(8,128)S(1)}, u32[]{:S(2)}, u32[]{:S(2)}) collective-permute-start(f32[1,2,1,64,256]{4,3,0,2,1:T(8,128)S(1)} %fusion.58), channel_id=1, source_target_pairs={{0,12},{2,14},{4,0},{6,2},{8,4},{10,6},{12,8},{14,10},{1,13},{3,15... | collective-permute-start | bytes 393224 | tf_op jit(solution)/shard_map/ppermute | solution.py:47
  84.3 0.2 collective-permute-start.3
  84.6 1.7 %collective-permute-start.4 = (f32[1,2,1,64,256]{4,3,0,2,1:T(8,128)S(1)}, f32[1,2,1,64,256]{4,3,0,2,1:T(8,128)S(1)}, u32[]{:S(2)}, u32[]{:S(2)}) collective-permute-start(f32[1,2,1,64,256]{4,3,0,2,1:T(8,128)S(1)} %get-tuple-element.14), channel_id=1, source_target_pairs={{0,8},{2,10},{4,12},{6,14},{8,0},{10,2},{12,4},{14,6},{1,9},{3,11}... | collective-permute-start | bytes 393224 | tf_op jit(solution)/shard_map/ppermute | solution.py:47
  86.3 1.6 %collective-permute-done.1 = f32[1,2,1,64,256]{4,3,0,2,1:T(8,128)S(1)} collective-permute-done((f32[1,2,1,64,256]{4,3,0,2,1:T(8,128)S(1)}, f32[1,2,1,64,256]{4,3,0,2,1:T(8,128)S(1)}, u32[]{:S(2)}, u32[]{:S(2)}) %collective-permute-start.1) | collective-permute-done | bytes 131104 | tf_op jit(solution)/shard_map/ppermute | solution.py:47
  87.9 0.6 collective-permute-start.5
  88.5 0.1 collective-permute-done.2
  88.6 6.1 %collective-permute-start.7 = (f32[1,2,1,64,256]{4,3,0,2,1:T(8,128)S(1)}, f32[1,2,1,64,256]{4,3,0,2,1:T(8,128)S(1)}, u32[]{:S(2)}, u32[]{:S(2)}) collective-permute-start(f32[1,2,1,64,256]{4,3,0,2,1:T(8,128)S(1)} %get-tuple-element.10), channel_id=1, source_target_pairs={{0,14},{2,0},{4,2},{6,4},{8,6},{10,8},{12,10},{14,12},{1,15},{3,1}... | collective-permute-start | bytes 393224 | tf_op jit(solution)/shard_map/ppermute | solution.py:47
  94.7 6.4 %collective-permute-done.3 = f32[1,2,1,64,256]{4,3,0,2,1:T(8,128)S(1)} collective-permute-done((f32[1,2,1,64,256]{4,3,0,2,1:T(8,128)S(1)}, f32[1,2,1,64,256]{4,3,0,2,1:T(8,128)S(1)}, u32[]{:S(2)}, u32[]{:S(2)}) %collective-permute-start.3) | collective-permute-done | bytes 131104 | tf_op jit(solution)/shard_map/ppermute | solution.py:47
  101.1 0.4 collective-permute-done.4
  101.5 0.0 collective-permute-done.5
  101.5 0.0 collective-permute-done.6
  101.6 0.0 collective-permute-done.7
  101.6 0.8 copy.11
  102.4 2.6 %gather_fusion.1 = f32[512,2,256]{2,1,0:T(2,128)S(1)} fusion(f32[2,512,256]{2,0,1:T(2,128)S(1)} %bitcast.102, s32[1024]{0:T(1024)S(1)} %pad_clamp_fusion), kind=kCustom, calls=%fused_computation.1 | custom fusion | bytes 2099200 | tf_op jit(solution)/shard_map/jit(_take)/gather | solution.py:80
  105.0 0.2 fusion.32
  105.2 0.1 multiply_subtract_fusion
  105.3 1.0 pad_maximum_fusion.2
  106.3 0.0 all-reduce.2.cloned.1.call-update
  106.3 23.5 %all-reduce.2.cloned.1.call-done = f32[2,512,256]{2,1,0:T(8,128)} async-done(((f32[2,512,256]{2,1,0:T(8,128)}), f32[2,512,256]{2,1,0:T(8,128)}) %all-reduce.2.cloned.1.call-update) | async-done | bytes 1048592 | tf_op jit(solution)/shard_map/psum | solution.py:87
  129.8 2.3 %copy.24 = f32[2,512,256]{2,1,0:T(8,128)} copy(f32[2,512,256]{2,1,0:T(8,128)} %all-reduce.2.cloned.1.call-done) | data formatting | bytes 2097152
  (17 shorter events, 0.2 us)
Async XLA Ops:
  6.5 123.3 %all-reduce.2.cloned.1.call-start = ((), (), s32[]{:S(2)}) async-start(), calls=%async_computation | async-start | bytes 2097152 | tf_op jit(solution)/shard_map/psum | solution.py:87
  6.5 4.6 %copy-start.4 = (bf16[2,1024,1024]{2,1,0:T(8,128)(2,1)S(1)}, bf16[2,1024,1024]{2,1,0:T(8,128)(2,1)}, u32[]{:S(2)}) copy-start(bf16[2,1024,1024]{2,1,0:T(8,128)(2,1)} %param.11) | copy-start | bytes 12582916
  6.5 4.6 %copy-start.6 = (bf16[1,2,512,1024]{3,2,1,0:T(8,128)(2,1)S(1)}, bf16[1,2,512,1024]{3,2,1,0:T(8,128)(2,1)}, u32[]{:S(2)}) copy-start(bf16[1,2,512,1024]{3,2,1,0:T(8,128)(2,1)} %param.8) | copy-start | bytes 6291460
  13.7 3.6 %copy-start.5 = (bf16[2,1024,1024]{2,1,0:T(8,128)(2,1)S(1)}, bf16[2,1024,1024]{2,1,0:T(8,128)(2,1)}, u32[]{:S(2)}) copy-start(bf16[2,1024,1024]{2,1,0:T(8,128)(2,1)} %param.11) | copy-start | bytes 12582916
  13.7 4.1 %copy-start.8 = (f32[512,1024]{1,0:T(8,128)S(1)}, f32[512,1024]{1,0:T(8,128)}, u32[]{:S(2)}) copy-start(f32[512,1024]{1,0:T(8,128)} %fusion) | copy-start | bytes 6291460
  19.2 4.6 %copy-start.2 = (s32[512]{0:T(512)S(1)}, s32[512]{0:T(512)}, u32[]{:S(2)}) copy-start(s32[512]{0:T(512)} %param.15) | copy-start | bytes 6148
  19.2 4.6 %copy-start.3 = (s32[1024]{0:T(1024)S(1)}, s32[1024]{0:T(1024)}, u32[]{:S(2)}) copy-start(s32[1024]{0:T(1024)} %param.10) | copy-start | bytes 12292
  19.2 9.2 %copy-start.7 = (s32[1,4]{1,0:T(1,128)S(1)}, s32[1,4]{1,0:T(1,128)}, u32[]{:S(2)}) copy-start(s32[1,4]{1,0:T(1,128)} %param.9) | copy-start | bytes 52
  19.7 49.9 %collective-permute-start = (bf16[2,512,512]{2,1,0:T(8,128)(2,1)S(1)}, bf16[2,512,512]{2,1,0:T(8,128)(2,1)}, u32[]{:S(2)}, u32[]{:S(2)}) collective-permute-start(bf16[2,512,512]{2,1,0:T(8,128)(2,1)S(1)} %get-tuple-element.5), channel_id=1, source_target_pairs={{0,8},{2,10},{4,12},{6,14},{8,0},{10,2},{12,4},{14,6},{1,9},{3,11}... | collective-permute-start | bytes 3145736 | tf_op jit(solution)/shard_map/ppermute | solution.py:23
  29.9 27.7 %copy-start.1 = (f32[16,2,256]{2,1,0:T(2,128)S(1)}, f32[16,2,256]{2,1,0:T(2,128)}, u32[]{:S(2)}) copy-start(f32[16,2,256]{2,1,0:T(2,128)} %param.14) | copy-start | bytes 98308
  74.2 1.3 copy-start
  78.7 9.2 %collective-permute-start.1 = (f32[1,2,1,64,256]{4,3,0,2,1:T(8,128)S(1)}, f32[1,2,1,64,256]{4,3,0,2,1:T(8,128)S(1)}, u32[]{:S(2)}, u32[]{:S(2)}) collective-permute-start(f32[1,2,1,64,256]{4,3,0,2,1:T(8,128)S(1)} %get-tuple-element.11), channel_id=1, source_target_pairs={{0,2},{2,4},{4,6},{6,8},{8,10},{10,12},{12,14},{14,0},{1,3},{3,5},... | collective-permute-start | bytes 393224 | tf_op jit(solution)/shard_map/ppermute | solution.py:47
  80.4 8.2 %collective-permute-start.2 = (f32[1,2,1,64,256]{4,3,0,2,1:T(8,128)S(1)}, f32[1,2,1,64,256]{4,3,0,2,1:T(8,128)S(1)}, u32[]{:S(2)}, u32[]{:S(2)}) collective-permute-start(f32[1,2,1,64,256]{4,3,0,2,1:T(8,128)S(1)} %get-tuple-element.12), channel_id=1, source_target_pairs={{0,4},{2,6},{4,8},{6,10},{8,12},{10,14},{12,0},{14,2},{1,5},{3,7},... | collective-permute-start | bytes 393224 | tf_op jit(solution)/shard_map/ppermute | solution.py:47
  81.0 20.5 %collective-permute-start.6 = (f32[1,2,1,64,256]{4,3,0,2,1:T(8,128)S(1)}, f32[1,2,1,64,256]{4,3,0,2,1:T(8,128)S(1)}, u32[]{:S(2)}, u32[]{:S(2)}) collective-permute-start(f32[1,2,1,64,256]{4,3,0,2,1:T(8,128)S(1)} %fusion.58), channel_id=1, source_target_pairs={{0,12},{2,14},{4,0},{6,2},{8,4},{10,6},{12,8},{14,10},{1,13},{3,15... | collective-permute-start | bytes 393224 | tf_op jit(solution)/shard_map/ppermute | solution.py:47
  84.3 16.7 %collective-permute-start.3 = (f32[1,2,1,64,256]{4,3,0,2,1:T(8,128)S(1)}, f32[1,2,1,64,256]{4,3,0,2,1:T(8,128)S(1)}, u32[]{:S(2)}, u32[]{:S(2)}) collective-permute-start(f32[1,2,1,64,256]{4,3,0,2,1:T(8,128)S(1)} %get-tuple-element.13), channel_id=1, source_target_pairs={{0,6},{2,8},{4,10},{6,12},{8,14},{10,0},{12,2},{14,4},{1,7},{3,9},... | collective-permute-start | bytes 393224 | tf_op jit(solution)/shard_map/ppermute | solution.py:47
  84.6 16.9 %collective-permute-start.4 = (f32[1,2,1,64,256]{4,3,0,2,1:T(8,128)S(1)}, f32[1,2,1,64,256]{4,3,0,2,1:T(8,128)S(1)}, u32[]{:S(2)}, u32[]{:S(2)}) collective-permute-start(f32[1,2,1,64,256]{4,3,0,2,1:T(8,128)S(1)} %get-tuple-element.14), channel_id=1, source_target_pairs={{0,8},{2,10},{4,12},{6,14},{8,0},{10,2},{12,4},{14,6},{1,9},{3,11}... | collective-permute-start | bytes 393224 | tf_op jit(solution)/shard_map/ppermute | solution.py:47
  87.9 13.6 %collective-permute-start.5 = (f32[1,2,1,64,256]{4,3,0,2,1:T(8,128)S(1)}, f32[1,2,1,64,256]{4,3,0,2,1:T(8,128)S(1)}, u32[]{:S(2)}, u32[]{:S(2)}) collective-permute-start(f32[1,2,1,64,256]{4,3,0,2,1:T(8,128)S(1)} %get-tuple-element.15), channel_id=1, source_target_pairs={{0,10},{2,12},{4,14},{6,0},{8,2},{10,4},{12,6},{14,8},{1,11},{3,13... | collective-permute-start | bytes 393224 | tf_op jit(solution)/shard_map/ppermute | solution.py:47
  88.6 12.9 %collective-permute-start.7 = (f32[1,2,1,64,256]{4,3,0,2,1:T(8,128)S(1)}, f32[1,2,1,64,256]{4,3,0,2,1:T(8,128)S(1)}, u32[]{:S(2)}, u32[]{:S(2)}) collective-permute-start(f32[1,2,1,64,256]{4,3,0,2,1:T(8,128)S(1)} %get-tuple-element.10), channel_id=1, source_target_pairs={{0,14},{2,0},{4,2},{6,4},{8,6},{10,8},{12,10},{14,12},{1,15},{3,1}... | collective-permute-start | bytes 393224 | tf_op jit(solution)/shard_map/ppermute | solution.py:47
Sparse Core Ops, SparseCore 0:
  106.5 23.3 all-reduce.1
